TPU v7x, 32 devices: a whole 2x2x4 slice. The times are simulated.
32 devices in a mesh: order: 4 (over z), degree: 2 (over y), site: 4 (over x, core).
Axes of the slice: x: 2, y: 2, z: 4, core: 2. Of those that a mesh axis runs over, the one named last changes fastest.
Arguments:
- scene_coeffs: bfloat16 [2, 16, 128, 256, 32], P(None, None, 'degree', 'order'), may hold values from -3 to 3
- site_ids: int32 [4], P('site'), may hold values from 0 to 31
- gripper_coeffs: bfloat16 [2, 16, 128, 256], P(None, None, 'degree', 'order'), may hold values from -3 to 3
- order_table: int32 [256], replicated, may hold values from 0 to 255, each once
- wigner: bfloat16 [128, 8, 256, 256], P('degree', None, 'order'), may hold values from -0.0029907227 to 0.0029907227
Outputs:
- scores: float32 [4, 8, 256, 256], P('site', 'degree', 'order')
Inputs may be any that keep to these rules, and one draw needn't show every extreme that they name: A permutation of the 256 slots; slot j holds order order_table[j] - 128. `site_ids`: sites may share a candidate.
All inputs are finite; a program needn't handle non-finite values.
Results may differ from a plain program's by a relative error of at most 0.0029.
Values may be sent and summed in bfloat16 or wider, within the bound.
A program may use at most 128 MiB of HBM per device.

v0:
```python
import math

import jax
import jax.numpy as jnp
from jax import lax
from jax.sharding import PartitionSpec as P


def shards(scene_coeffs, site_ids, gripper_coeffs, order_table, wigner):
    highest = lax.Precision.HIGHEST
    slot_count = order_table.shape[0]
    local_deg = gripper_coeffs.shape[2]
    local_ord = gripper_coeffs.shape[3]
    cand_count = scene_coeffs.shape[4]
    site_count = site_ids.shape[0]
    order_pos = lax.axis_index("order")
    degree_pos = lax.axis_index("degree")
    orders = order_table - slot_count // 2
    angles = jnp.arange(slot_count, dtype=jnp.int32)
    phase_index = jnp.mod(orders[:, None] * angles[None, :], slot_count)
    radians = phase_index.astype(jnp.float32) * (2.0 * math.pi / slot_count)
    cosine = jnp.cos(radians)
    sine_table = jnp.sin(radians)
    magnitude = jnp.abs(orders)
    resident_degrees = degree_pos * local_deg + jnp.arange(local_deg, dtype=jnp.int32)
    owned_orders = lax.dynamic_slice_in_dim(magnitude, order_pos * local_ord, local_ord)
    grip_allowed = owned_orders[None, :] <= resident_degrees[:, None]
    selector = (jnp.arange(cand_count, dtype=jnp.int32)[:, None] == site_ids[None, :]).astype(
        jnp.bfloat16
    )
    chosen = jnp.dot(
        scene_coeffs.reshape(-1, cand_count), selector, preferred_element_type=jnp.float32
    )
    chosen = chosen.astype(jnp.bfloat16).reshape(
        2, scene_coeffs.shape[1], local_deg, local_ord, site_count
    )
    grip_real = jnp.concatenate([gripper_coeffs[0], gripper_coeffs[1]], axis=0)
    grip_imag = jnp.concatenate([-gripper_coeffs[1], gripper_coeffs[0]], axis=0)
    gripper_couple = jnp.stack([grip_real, grip_imag])
    columns_in = lax.all_gather(chosen, "order", axis=3, tiled=True)
    scene_joined = jnp.concatenate([columns_in[0], columns_in[1]], axis=0)
    product = jnp.einsum(
        "aonw,iaob->iobnw", scene_joined, gripper_couple, preferred_element_type=jnp.float32
    )
    permitted_mask = grip_allowed[:, :, None] & (
        magnitude[None, None, :] <= resident_degrees[:, None, None]
    )
    product = jnp.where(permitted_mask[None, :, :, :, None], product, jnp.float32(0.0)).astype(
        jnp.bfloat16
    )
    partial_value = jnp.einsum(
        "ylprs,lbpr->ysbpr", product, wigner, preferred_element_type=jnp.float32
    )
    summed = lax.psum_scatter(partial_value, "degree", scatter_dimension=2, tiled=True)
    phase_pair = jnp.concatenate([cosine, sine_table], axis=1)
    products = jnp.einsum(
        "xsbpm,mk->xsbpk", summed, phase_pair, precision=highest, preferred_element_type=jnp.float32
    )
    real_alpha = products[0, ..., :slot_count] - products[1, ..., slot_count:]
    imag_alpha = products[0, ..., slot_count:] + products[1, ..., :slot_count]
    stacked_parts = jnp.stack([real_alpha, imag_alpha])
    exchanged = lax.all_to_all(stacked_parts, "order", split_axis=4, concat_axis=3, tiled=True)
    first_term = jnp.einsum(
        "sbpa,pk->sbak", exchanged[0], cosine, precision=highest, preferred_element_type=jnp.float32
    )
    latter_addend = jnp.einsum(
        "sbpa,pk->sbak",
        exchanged[1],
        sine_table,
        precision=highest,
        preferred_element_type=jnp.float32,
    )
    return first_term - latter_addend


def solution(mesh):
    in_specs = (
        P(None, None, "degree", "order", None),
        P("site"),
        P(None, None, "degree", "order"),
        P(),
        P("degree", None, "order", None),
    )
    out_specs = P("site", "degree", "order", None)
    return jax.shard_map(shards, mesh=mesh, in_specs=in_specs, out_specs=out_specs, check_vma=False)
```

profile of v0, /device:TPU:0, one launch (start us, length us, event | category | flops | bytes accessed | tf_op | source)
XLA Modules:
  0.0 215.1 jit_solution(12840888628836542837)
XLA Ops:
  6.5 15.2 %copy.27 = bf16[2,16,64,64,32]{3,2,1,0,4:T(8,128)(2,1)} copy(bf16[2,16,64,64,32]{3,4,2,1,0:T(8,128)(2,1)} %param.5) | data formatting | bytes 16777216 | tf_op args[0]
  21.7 16.0 %reshape.133 = bf16[131072,32]{0,1:T(8,128)(2,1)} reshape(bf16[2,16,64,64,32]{3,2,1,0,4:T(8,128)(2,1)} %copy.27) | data formatting | bytes 16777216 | tf_op jit(solution)/shard_map/reshape | solution.py:32
  38.4 4.6 %fusion.24 = f32[1,131072]{1,0:T(1,128)S(1)} fusion(bf16[131072,32]{0,1:T(8,128)(2,1)} %reshape.133, s32[]{:T(128)} %bitcast.75), kind=kOutput, calls=%fused_computation.42 | convolution fusion | flops 8388640 | bytes 8912900 | tf_op jit(solution)/shard_map/dot_general | solution.py:31
  43.3 1.5 copy.28
  45.1 33.5 %copy.32 = bf16[64,8,64,256]{0,1,3,2:T(8,128)(2,1)} copy(bf16[64,8,64,256]{3,2,1,0:T(8,128)(2,1)} %param.9) | data formatting | bytes 33554432 | tf_op args[4]
  79.2 1.2 maximum_bitcast_fusion.2
  80.6 1.0 broadcast_and_fusion
  81.6 11.7 %all-gather.2.cloned.1.call-done = bf16[2,16,64,256,1]{2,1,4,0,3:T(8,128)(2,1)} async-done(((bf16[2,16,64,64,1]{2,1,4,0,3:T(8,128)(2,1)}), bf16[2,16,64,256,1]{2,1,4,0,3:T(8,128)(2,1)}) %all-gather.2.cloned.1.call-update) | async-done | bytes 1048592 | tf_op jit(solution)/shard_map/all_gather | solution.py:40
  93.3 1.9 fusion.40
  95.2 2.2 %copy.41 = bf16[1,16,64,256,1]{3,1,2,4,0:T(8,128)(2,1)} copy(bf16[1,16,64,256,1]{2,1,4,0,3:T(8,128)(2,1)S(1)} %get-tuple-element.5) | data formatting | bytes 1048576
  97.4 1.3 copy.42
  98.7 4.9 %fusion.1 = bf16[2,64,64,256]{3,2,0,1:T(8,128)(2,1)} fusion(pred[64,64,256]{2,1,0:T(8,128)(4,1)S(1)} %broadcast_and_fusion, bf16[1,32,64,64]{3,1,0,2:T(8,128)(2,1)} %get-tuple-element.14, bf16[1,32,64,64]{3,1,0,2:T(8,128)(2,1)} %get-tuple-element.13, bf16[16,64,256,1]{2,0,1,3:T(8,128)(2,1)S(1)} %bitcast.81, bf16[16,64,256,1]{2,0,1,3:T(8,128)(2,1)} %bitcast.80), kind=kOutput, calls=%fused_computation.3 | convolution fusion | flops 140771328 | bytes 6815744 | tf_op jit(solution)/shard_map/aonw,iaob->iobnw/dot_general | solution.py:42
  103.7 14.5 %copy.31 = bf16[2,64,64,256]{1,0,3,2:T(2,128)(2,1)} copy(bf16[2,64,64,256]{3,2,0,1:T(8,128)(2,1)} %fusion.1) | data formatting | bytes 8388608 | tf_op jit(solution)/shard_map/reshape.10
  118.2 25.7 %convolution_bitcast_fusion = f32[2,1,8,64,256]{2,0,4,3,1:T(2,128)} fusion(bf16[2,64,64,256]{1,0,3,2:T(2,128)(2,1)} %copy.31, bf16[64,8,64,256]{0,1,3,2:T(8,128)(2,1)} %copy.32), kind=kOutput, calls=%fused_computation | convolution fusion | flops 33554432 | bytes 22020096 | tf_op jit(solution)/shard_map/ylprs,lbpr->ysbpr/dot_general | solution.py:51
  143.9 14.2 %copy.33 = f32[2,1,8,64,256]{4,3,1,0,2:T(8,128)} copy(f32[2,1,8,64,256]{2,0,4,3,1:T(2,128)} %convolution_bitcast_fusion) | data formatting | bytes 2097152 | tf_op jit(solution)/shard_map/ylprs,lbpr->ysbpr/transpose | solution.py:51
  158.2 1.1 fusion.21
  159.3 18.3 %reduce-scatter.2.cloned.1.call-done = f32[2,1,4,64,256]{4,3,1,0,2:T(8,128)} async-done(((f32[2,1,8,64,256]{4,3,1,0,2:T(8,128)}), f32[2,1,4,64,256]{4,3,1,0,2:T(8,128)}) %reduce-scatter.2.cloned.1.call-update) | async-done | bytes 524304 | tf_op jit(solution)/shard_map/reduce_scatter | solution.py:54
  177.5 2.0 convolution_bitcast_fusion.1
  180.2 1.0 reshape.146
  181.2 18.7 %all_to_all.15 = f32[4,1,32768]{2,1,0:T(1,128)S(1)} all-to-all(f32[4,1,32768]{2,1,0:T(1,128)S(1)} %reshape.146), channel_id=1, replica_groups=mesh['order'=4,'degree'=2,'site'=4] {'order'}, dimensions={0} | all-to-all | bytes 1048576 | tf_op jit(solution)/shard_map/all_to_all | solution.py:62
  200.4 2.1 reduce
  202.6 0.7 reshape.147
  204.4 1.4 fusion.15
  206.1 2.1 fusion.2
  (26 shorter events, 3.9 us)
Async XLA Ops:
  6.5 86.8 %all-gather.2.cloned.1.call-start = ((), (), s32[]{:S(2)}) async-start(), calls=%async_computation.2 | async-start | bytes 2621440 | tf_op jit(solution)/shard_map/all_gather | solution.py:40
  37.7 7.3 %copy-start.1 = (s32[256]{0:T(256)S(1)}, s32[256]{0:T(256)}, u32[]{:S(2)}) copy-start(s32[256]{0:T(256)} %param.8) | copy-start | bytes 3076
  44.8 132.7 %reduce-scatter.2.cloned.1.call-start = ((), (), s32[]{:S(2)}) async-start(), calls=%async_computation.3 | async-start | bytes 1572864 | tf_op jit(solution)/shard_map/reduce_scatter | solution.py:54
  45.1 33.6 %copy-start = (bf16[2,16,64,64]{3,2,1,0:T(8,128)(2,1)S(1)}, bf16[2,16,64,64]{3,2,1,0:T(8,128)(2,1)}, u32[]{:S(2)}) copy-start(bf16[2,16,64,64]{3,2,1,0:T(8,128)(2,1)} %param.7) | copy-start | bytes 786436
Sparse Core Ops, SparseCore 0:
  44.9 48.3 all-gather.1
  158.3 19.1 reduce-scatter.1
where the time goes:
time: 217 us; the launch traced here: 215 us
  local copies, waits for them, and re-layouts  105 us (48%)
  matrix products  40.9 us (19%)
  waiting for transfers between devices  30 us (14%)
  blocking collectives  18.7 us (9%)
  between operations  14.3 us (7%)
  other arithmetic  5.92 us (3%)
    unnamed x10, local copies, waits for them, and re-layouts  53.9 us
    dot_general x1, matrix products, shards(): jnp.einsum('ylprs,lbpr->ysbpr', product, wigner, preferred_element_type=j...  25.7 us
    all_to_all x1, blocking collectives, shards(): lax.all_to_all(stacked_parts, 'order', split_axis=4, concat_axis=3, tiled...  18.7 us
    reduce_scatter x1, waiting for transfers between devices, shards(): lax.psum_scatter(partial_value, 'degree', scatter_dimension=2, tiled=True)  18.3 us
    reshape x1, local copies, waits for them, and re-layouts, shards(): scene_coeffs.reshape(-1, cand_count)  16 us
    another operation x3, local copies, waits for them, and re-layouts  15.2 us
    transpose x1, local copies, waits for them, and re-layouts, shards(): jnp.einsum('ylprs,lbpr->ysbpr', product, wigner, preferred_element_type=j...  14.2 us
    all_gather x1, waiting for transfers between devices, shards(): columns_in = lax.all_gather(chosen, 'order', axis=3, tiled=True)  11.7 us
  transfers between devices with their start and end apart: 2, of which 2 were waited for; matrix products, arithmetic and copies ran while one was open for 17% of the time, Pallas kernels for 0%

commit v1 on v0

--- a/solution.py
+++ b/solution.py
@@ -3,10 +3,12 @@
 import jax
 import jax.numpy as jnp
 from jax import lax
+from jax.experimental import pallas as pl
+from jax.experimental.pallas import tpu as pltpu
 from jax.sharding import PartitionSpec as P
 
 
-def shards(scene_coeffs, site_ids, gripper_coeffs, order_table, wigner):
+def general_shards(scene_coeffs, site_ids, gripper_coeffs, order_table, wigner):
     highest = lax.Precision.HIGHEST
     slot_count = order_table.shape[0]
     local_deg = gripper_coeffs.shape[2]
@@ -73,7 +75,250 @@
     return first_term - latter_addend
 
 
+MESH = pl.DeviceIdType.MESH
+F32, BF16 = jnp.float32, jnp.bfloat16
+CHUNKS = 4
+
+
+def cos_of(index, count):
+    centred = jnp.bitwise_and(index + count // 2, count - 1) - count // 2
+    half = centred.astype(F32) * F32(math.pi / count)
+    sq = half * half
+    poly = F32(-1.0 / 39916800.0)
+    for coefficient in (1.0 / 362880.0, -1.0 / 5040.0, 1.0 / 120.0, -1.0 / 6.0, 1.0):
+        poly = poly * sq + F32(coefficient)
+    sine = poly * half
+    return 1.0 - 2.0 * sine * sine
+
+
+def split(value):
+    high = value.astype(BF16)
+    return high, (value - high.astype(F32)).astype(BF16)
+
+
+def fused_kernel(
+    s_ref, g_ref, col_ref, row_ref, w_ref, out_ref,
+    wbuf, sbuf, prod, accbuf, rs_send, rs_recv, a_send, a_recv, halfacc,
+    alpha_hi, alpha_lo, gamma_hi, gamma_lo,
+    w_sem, s_send_sem, s_recv_sem, r_send_sem, r_recv_sem, x_send_sem, x_recv_sem,
+):
+    me = lax.axis_index("order")
+    deg = lax.axis_index("degree")
+    L, NBETA, P, M = wbuf.shape[1:]
+    SL = 2 * M
+    BO = NBETA // 2
+    first = me // 2
+    second = 1 - first
+    per = L // CHUNKS
+
+    def w_copy(h, c):
+        return pltpu.make_async_copy(
+            w_ref.at[pl.ds(c * per, per), :, :, pl.ds(pl.multiple_of(h * M, M), M)],
+            wbuf.at[h, pl.ds(c * per, per)],
+            w_sem.at[h, c],
+        )
+
+    for h in (first, second):
+        for c in range(CHUNKS):
+            w_copy(h, c).start()
+
+    barrier = pltpu.get_barrier_semaphore()
+    for off in (1, 2, 3):
+        pl.semaphore_signal(barrier, 1, device_id={"order": (me + off) % 4}, device_id_type=MESH)
+    pl.semaphore_signal(barrier, 1, device_id={"degree": 1 - deg}, device_id_type=MESH)
+    pl.semaphore_wait(barrier, 4)
+
+    def s_copy(target, slot, off):
+        return pltpu.make_async_remote_copy(
+            src_ref=s_ref, dst_ref=sbuf.at[slot],
+            send_sem=s_send_sem.at[off], recv_sem=s_recv_sem.at[off],
+            device_id={"order": target}, device_id_type=MESH,
+        )
+
+    for off in (1, 3, 2):
+        s_copy((me + off) % 4, me, off).start()
+
+    def s_wait(source):
+        off = (me - source + 4) % 4
+        s_copy(source, source, off).wait_recv()
+
+    sbuf[me] = s_ref[...]
+
+    ang = lax.broadcasted_iota(jnp.int32, (M, 2 * SL), 1)
+    tgt = (ang // 128) * P + ang % P
+    part = (ang // P) % 2
+    quarter = SL // 4
+    for h in range(2):
+        orders = col_ref[h * M : (h + 1) * M, :] - SL // 2
+        for x in range(2):
+            table = cos_of(orders * tgt + (x - part) * quarter, SL)
+            hi, lo = split(table)
+            alpha_hi[h, x * M : (x + 1) * M, :] = hi
+            alpha_lo[h, x * M : (x + 1) * M, :] = lo
+        table = cos_of(orders * (ang % SL) + (ang // SL) * quarter, SL)
+        hi, lo = split(table)
+        gamma_hi[h * M : (h + 1) * M, :] = hi
+        gamma_lo[h * M : (h + 1) * M, :] = lo
+
+    mag_p = jnp.abs(col_ref[pl.ds(pl.multiple_of(me * P, P), P), :] - SL // 2)
+    dims = (((0,), (0,)), ((), ()))
+
+    def compute(h):
+        mag_m = jnp.abs(row_ref[h] - SL // 2)
+        most = jnp.maximum(jnp.broadcast_to(mag_p, (P, M)), jnp.broadcast_to(mag_m, (P, M)))
+        most = jnp.concatenate([most, most], axis=0)
+
+        def product(step, carry):
+            b0, b1 = sbuf[2 * h, step], sbuf[2 * h + 1, step]
+            low = jnp.concatenate([b0[:, :P], b1[:, :P]], axis=1)
+            high = jnp.concatenate([b0[:, P:], b1[:, P:]], axis=1)
+            for l, scene in ((step, low), (step + L // 2, high)):
+                value = lax.dot_general(g_ref[l], scene, dims, preferred_element_type=F32)
+                value = jnp.where(most <= deg * L + l, value, F32(0.0))
+                prod[l] = value.astype(BF16)
+            return carry
+
+        lax.fori_loop(0, L // 2, product, 0)
+        for c in range(CHUNKS):
+            w_copy(h, c).wait()
+
+        ROWS = 16
+
+        def rows(blk, carry):
+            at = pl.multiple_of(blk * ROWS, ROWS)
+
+            def degree_step(l, acc):
+                pr = prod[l, pl.ds(at, ROWS), :].astype(F32)
+                pi = prod[l, pl.ds(at + P, ROWS), :].astype(F32)
+                new = []
+                for b in range(NBETA):
+                    w = wbuf[h, l, b, pl.ds(at, ROWS), :].astype(F32)
+                    new.append(acc[2 * b] + pr * w)
+                    new.append(acc[2 * b + 1] + pi * w)
+                return tuple(new)
+
+            zero = jnp.zeros((ROWS, M), F32)
+            acc = lax.fori_loop(0, L, degree_step, (zero,) * (2 * NBETA), unroll=2)
+            for b in range(NBETA):
+                accbuf[h, b, 0, pl.ds(at, ROWS), :] = acc[2 * b]
+                accbuf[h, b, 1, pl.ds(at, ROWS), :] = acc[2 * b + 1]
+            return carry
+
+        lax.fori_loop(0, P // ROWS, rows, 0)
+        rs_send[h] = accbuf[h, pl.ds((1 - deg) * BO, BO)].astype(BF16)
+
+    def r_copy(h):
+        return pltpu.make_async_remote_copy(
+            src_ref=rs_send.at[h], dst_ref=rs_recv.at[h],
+            send_sem=r_send_sem.at[h], recv_sem=r_recv_sem.at[h],
+            device_id={"degree": 1 - deg}, device_id_type=MESH,
+        )
+
+    def alpha(h):
+        r_copy(h).wait_recv()
+        total = accbuf[h, pl.ds(deg * BO, BO)] + rs_recv[h].astype(F32)
+        total = jnp.concatenate(
+            [total[:, 0].reshape(BO * P, M), total[:, 1].reshape(BO * P, M)], axis=1
+        )
+        hi, lo = split(total)
+        value = jnp.dot(hi, alpha_hi[h], preferred_element_type=F32)
+        value += jnp.dot(hi, alpha_lo[h], preferred_element_type=F32)
+        value += jnp.dot(lo, alpha_hi[h], preferred_element_type=F32)
+        return value
+
+    s_wait(first * 2 + (1 - me % 2))
+    compute(first)
+    r_copy(first).start()
+    s_wait(second * 2 + (1 - first))
+    s_wait(second * 2 + first)
+    compute(second)
+    r_copy(second).start()
+    halfacc[...] = alpha(first)
+    value = (halfacc[...] + alpha(second)).astype(BF16)
+    for t in range(4):
+        a_send[t] = value[:, t * 128 : (t + 1) * 128]
+
+    def x_copy(target, source, off):
+        return pltpu.make_async_remote_copy(
+            src_ref=a_send.at[target], dst_ref=a_recv.at[source],
+            send_sem=x_send_sem.at[off], recv_sem=x_recv_sem.at[off],
+            device_id={"order": target}, device_id_type=MESH,
+        )
+
+    for off in (2, 1, 3):
+        x_copy((me + off) % 4, me, off).start()
+    a_recv[me] = a_send[me]
+    for off in (1, 3, 2):
+        source = (me - off + 4) % 4
+        x_copy(source, source, off).wait_recv()
+
+    for b in range(BO):
+        got = jnp.concatenate([a_recv[z, b * P : (b + 1) * P, :] for z in range(4)], axis=0)
+        score = jnp.zeros((P, SL), F32)
+        for x in range(2):
+            for table in (gamma_hi, gamma_lo):
+                score += lax.dot_general(
+                    got[:, x * P : (x + 1) * P], table[:, x * SL : (x + 1) * SL], dims,
+                    preferred_element_type=F32,
+                )
+        out_ref[0, b] = score
+
+    for off in (1, 2, 3):
+        s_copy((me + off) % 4, me, off).wait_send()
+        x_copy((me + off) % 4, me, off).wait_send()
+    r_copy(first).wait_send()
+    r_copy(second).wait_send()
+
+
+def fused_shards(scene_coeffs, site_ids, gripper_coeffs, order_table, wigner):
+    L, NBETA, P, SL = wigner.shape
+    M = SL // 2
+    K = 2 * scene_coeffs.shape[1]
+    chosen = lax.dynamic_index_in_dim(scene_coeffs, site_ids[0], axis=4, keepdims=False)
+    s = jnp.transpose(chosen, (2, 0, 1, 3)).reshape(2, L // 2, K, P)
+    s = jnp.concatenate([s[0], s[1]], axis=-1)
+    couple = jnp.concatenate(
+        [gripper_coeffs, jnp.stack([-gripper_coeffs[1], gripper_coeffs[0]])], axis=-1
+    )
+    g = jnp.transpose(couple, (2, 0, 1, 3)).reshape(L, K, 2 * P)
+    vmem = pl.BlockSpec(memory_space=pltpu.VMEM)
+    BO = NBETA // 2
+    return pl.pallas_call(
+        fused_kernel,
+        out_shape=jax.ShapeDtypeStruct((1, BO, P, SL), F32),
+        in_specs=[vmem, vmem, vmem, vmem, pl.BlockSpec(memory_space=pl.ANY)],
+        out_specs=vmem,
+        scratch_shapes=[
+            pltpu.VMEM((2, L, NBETA, P, M), BF16),
+            pltpu.VMEM((4, L // 2, K, 2 * P), BF16),
+            pltpu.VMEM((L, 2 * P, M), BF16),
+            pltpu.VMEM((2, NBETA, 2, P, M), F32),
+            pltpu.VMEM((2, BO, 2, P, M), BF16),
+            pltpu.VMEM((2, BO, 2, P, M), BF16),
+            pltpu.VMEM((4, BO * P, 128), BF16),
+            pltpu.VMEM((4, BO * P, 128), BF16),
+            pltpu.VMEM((BO * P, 2 * SL), F32),
+            pltpu.VMEM((2, 2 * M, 2 * SL), BF16),
+            pltpu.VMEM((2, 2 * M, 2 * SL), BF16),
+            pltpu.VMEM((SL, 2 * SL), BF16),
+            pltpu.VMEM((SL, 2 * SL), BF16),
+            pltpu.SemaphoreType.DMA((2, CHUNKS)),
+            pltpu.SemaphoreType.DMA((4,)),
+            pltpu.SemaphoreType.DMA((4,)),
+            pltpu.SemaphoreType.DMA((2,)),
+            pltpu.SemaphoreType.DMA((2,)),
+            pltpu.SemaphoreType.DMA((4,)),
+            pltpu.SemaphoreType.DMA((4,)),
+        ],
+        compiler_params=pltpu.CompilerParams(
+            collective_id=0, has_side_effects=True, vmem_limit_bytes=48 * 1024 * 1024
+        ),
+    )(s, g, order_table.reshape(SL, 1), order_table.reshape(2, 1, M), wigner)
+
+
 def solution(mesh):
+    fits = mesh.shape["order"] == 4 and mesh.shape["degree"] == 2 and mesh.shape["site"] == 4
+    shards = fused_shards if fits else general_shards
     in_specs = (
         P(None, None, "degree", "order", None),
         P("site"),

time: 217 us -> 61.5 us (0.28)
  local copies, waits for them, and re-layouts: 105 us -> 6.37 us
  Pallas kernels: 0 us -> 51.6 us
  matrix products: 40.9 us -> 0 us
  waiting for transfers between devices: 30 us -> 0 us
  blocking collectives: 18.7 us -> 0 us
  between operations: 14.3 us -> 0.74 us
  other arithmetic: 5.92 us -> 2.57 us
    unnamed x10 -> x4, local copies, waits for them, and re-layouts: 53.9 us -> 1.46 us
    pallas_call x0 -> x1, Pallas kernels: none -> 51.6 us  [fused_shards(): pl.pallas_call(fused_kernel, out_shape=jax.ShapeDtypeStruct((1, BO, P, SL...]
    dot_general x6 -> x0, matrix products: 40.9 us -> none  [the longest x1 25.7 us: shards(): jnp.einsum('ylprs,lbpr->ysbpr', product, wigner, preferred_element_type=j...]
    all_to_all x1 -> x0, blocking collectives: 18.7 us -> none  [shards(): lax.all_to_all(stacked_parts, 'order', split_axis=4, concat_axis=3, tiled...]
    reduce_scatter x1 -> x0, waiting for transfers between devices: 18.3 us -> none  [shards(): lax.psum_scatter(partial_value, 'degree', scatter_dimension=2, tiled=True)]
    reshape x3 -> x1, local copies, waits for them, and re-layouts: 17.7 us -> 0.81 us  [fused_shards(): order_table.reshape(SL, 1)]
    another operation x4 -> x0, local copies, waits for them, and re-layouts: 15.7 us -> none
    transpose x1, local copies, waits for them, and re-layouts: 14.2 us -> 0.34 us  [fused_shards(): g = jnp.transpose(couple, (2, 0, 1, 3)).reshape(L, K, 2 * P)]
  transfers between devices with their start and end apart: 2 -> 0, of which waited for: 2 -> 0; matrix products, arithmetic and copies ran while one was open for 17% -> 0% of each run, Pallas kernels for 0% -> 0%
where the time goes in v1:
time: 61.5 us; the launch traced here: 61.3 us
  Pallas kernels  51.6 us (84%)
  local copies, waits for them, and re-layouts  6.37 us (10%)
  other arithmetic  2.57 us (4%)
  between operations  0.74 us (1%)
    pallas_call x1, Pallas kernels, fused_shards(): pl.pallas_call(fused_kernel, out_shape=jax.ShapeDtypeStruct((1, BO, P, SL...  51.6 us
    dynamic_slice x1, local copies, waits for them, and re-layouts, fused_shards(): lax.dynamic_index_in_dim(scene_coeffs, site_ids[0], axis=4, keepdims=False)  3.51 us
    unnamed x4, local copies, waits for them, and re-layouts  1.46 us
    transpose x1, other arithmetic, fused_shards(): g = jnp.transpose(couple, (2, 0, 1, 3)).reshape(L, K, 2 * P)  1.34 us

profile of v1, /device:TPU:0, one launch (start us, length us, event | category | flops | bytes accessed | tf_op | source)
XLA Modules:
  0.0 61.3 jit_solution(3742446295264090152)
XLA Ops:
  0.7 3.5 %constant_dynamic-slice_fusion = bf16[2,16,64,64,1]{3,4,2,1,0:T(2,128)(2,1)S(1)} fusion(bf16[2,16,64,64,32]{3,4,2,1,0:T(8,128)(2,1)} %param.5, s32[]{:T(128)S(6)} %select_n.4), kind=kLoop, calls=%fused_computation.4 | loop fusion | bytes 524292 | tf_op jit(solution)/shard_map/jit(dynamic_index_in_dim)/dynamic_slice | solution.py:277
  4.2 0.1 copy.14
  4.3 0.1 copy.8
  4.4 0.1 copy.9
  4.5 0.1 pad_maximum_fusion.s_ref
  4.7 1.1 %slice_negate_fusion = (bf16[1,16,64,64]{3,2,1,0:T(8,128)(2,1)S(1)}, bf16[1,16,64,64]{3,2,1,0:T(8,128)(2,1)S(1)}) fusion(bf16[2,16,64,64]{3,2,1,0:T(8,128)(2,1)} %param.7), kind=kLoop, calls=%fused_computation.3 | loop fusion | flops 65536 | bytes 524288 | tf_op jit(solution)/shard_map/neg | solution.py:281
  5.8 1.3 %maximum_bitcast_fusion = bf16[64,2,16,128]{3,0,2,1:T(8,128)(2,1)S(1)} fusion(bf16[1,16,64,64]{3,2,1,0:T(8,128)(2,1)S(1)} %get-tuple-element.6, bf16[1,16,64,64]{3,2,1,0:T(8,128)(2,1)S(1)} %get-tuple-element.5, bf16[2,16,64,64]{3,2,1,0:T(8,128)(2,1)} %param.7), kind=kLoop, calls=%fused_computation | loop fusion | flops 1572864 | bytes 1048576 | tf_op jit(solution)/shard_map/transpose | solution.py:283
  7.1 0.3 copy.10
  7.5 0.8 %copy.11.col_ref = s32[256,1]{1,0:T(8,128)S(1)} copy(s32[256,1]{0,1:T(1,128)} %bitcast.17) | data formatting | bytes 2048 | tf_op jit(solution)/shard_map/reshape | solution.py:316
  8.3 0.0 copy-start
  8.3 0.7 %copy-done = s32[256]{0:T(256)S(1)} copy-done((s32[256]{0:T(256)S(1)}, s32[256]{0:T(256)}, u32[]{:S(2)}) %copy-start) | copy-done | bytes 1048
  9.0 51.6 %shard_map.55 = f32[1,4,64,256]{3,2,1,0:T(8,128)S(1)} custom-call(bf16[32,32,128]{2,1,0:T(8,128)(2,1)S(1)} %pad_maximum_fusion.s_ref, bf16[64,32,128]{2,1,0:T(8,128)(2,1)S(1)} %bitcast.16, s32[256,1]{1,0:T(8,128)S(1)} %copy.11.col_ref, s32[2,1,128]{2,1,0:T(1,128)S(1)} %bitcast.18, bf16[64,8,64,256]{3,2,1,0:T(8,128)(2,1)} %w_ref.1), custom_call_target="tpu_custom_call" | custom-call | tf_op jit(solution)/shard_map/pallas_call | solution.py:286
  60.5 0.7 %copy.17 = f32[1,4,64,256]{3,2,1,0:T(8,128)} copy(f32[1,4,64,256]{3,2,1,0:T(8,128)S(1)} %shard_map.55) | data formatting | bytes 524288
  (1 shorter events, 0.0 us)
Async XLA Ops:
  8.3 0.7 %copy-start = (s32[256]{0:T(256)S(1)}, s32[256]{0:T(256)}, u32[]{:S(2)}) copy-start(s32[256]{0:T(256)} %param.8) | copy-start | bytes 3076

commit v2 on v0

--- a/solution.py
+++ b/solution.py
@@ -3,10 +3,12 @@
 import jax
 import jax.numpy as jnp
 from jax import lax
+from jax.experimental import pallas as pl
+from jax.experimental.pallas import tpu as pltpu
 from jax.sharding import PartitionSpec as P
 
 
-def shards(scene_coeffs, site_ids, gripper_coeffs, order_table, wigner):
+def general_shards(scene_coeffs, site_ids, gripper_coeffs, order_table, wigner):
     highest = lax.Precision.HIGHEST
     slot_count = order_table.shape[0]
     local_deg = gripper_coeffs.shape[2]
@@ -73,7 +75,322 @@
     return first_term - latter_addend
 
 
+MESH = pl.DeviceIdType.MESH
+F32, BF16 = jnp.float32, jnp.bfloat16
+CHUNKS = 4
+ROWS = 16
+
+
+def cos_of(index, count):
+    centred = jnp.bitwise_and(index + count // 2, count - 1) - count // 2
+    half = centred.astype(F32) * F32(math.pi / count)
+    sq = half * half
+    poly = F32(-1.0 / 39916800.0)
+    for coefficient in (1.0 / 362880.0, -1.0 / 5040.0, 1.0 / 120.0, -1.0 / 6.0, 1.0):
+        poly = poly * sq + F32(coefficient)
+    sine = poly * half
+    return 1.0 - 2.0 * sine * sine
+
+
+def split(value):
+    high = value.astype(BF16)
+    return high, (value - high.astype(F32)).astype(BF16)
+
+
+def fused_kernel(
+    s_ref, g_ref, row_ref, w_ref, out_ref,
+    wbuf, sbuf, prod, accbuf, rs_send, rs_recv, a_send, a_recv, halfacc,
+    alpha_hi, alpha_lo, gamma_hi, gamma_lo, g32, col,
+    w_sem, s_send_sem, s_recv_sem, r_send_sem, r_recv_sem, x_send_sem, x_recv_sem,
+):
+    me = lax.axis_index("order")
+    deg = lax.axis_index("degree")
+    HL, NBETA, P, M = wbuf.shape[2:]
+    L = 2 * HL
+    SL = 2 * M
+    BO = NBETA // 2
+    K = s_ref.shape[1]
+    first = me // 2
+    second = 1 - first
+    near = first * 2 + (1 - me % 2)
+    per = HL // CHUNKS
+    blocks = P // ROWS
+
+    def w_copy(h, c):
+        return pltpu.make_async_copy(
+            w_ref.at[:, pl.ds(c * per, per), :, :, pl.ds(pl.multiple_of(h * M, M), M)],
+            wbuf.at[h, :, pl.ds(c * per, per)],
+            w_sem.at[h, c],
+        )
+
+    barrier = pltpu.get_barrier_semaphore()
+    for off in (1, 2, 3):
+        pl.semaphore_signal(barrier, 1, device_id={"order": (me + off) % 4}, device_id_type=MESH)
+    pl.semaphore_signal(barrier, 1, device_id={"degree": 1 - deg}, device_id_type=MESH)
+
+    for h in (first, second):
+        for c in range(CHUNKS):
+            w_copy(h, c).start()
+
+    pl.semaphore_wait(barrier, 4)
+
+    def hop(block, c, way, own=False):
+        rows = pl.ds(c * per, per)
+        return pltpu.make_async_remote_copy(
+            src_ref=s_ref.at[rows] if own else sbuf.at[block, rows],
+            dst_ref=sbuf.at[block, rows],
+            send_sem=s_send_sem.at[way, block, c], recv_sem=s_recv_sem.at[block, c],
+            device_id={"order": me + 1 - 2 * way}, device_id_type=MESH,
+        )
+
+    for c in range(CHUNKS):
+        @pl.when(me < 3)
+        def _():
+            hop(me, c, 0, True).start()
+
+        @pl.when(me > 0)
+        def _():
+            hop(me, c, 1, True).start()
+
+    sbuf[me] = s_ref[...]
+
+    for h in range(2):
+        line = jnp.broadcast_to(row_ref[h].astype(F32), (M, M))
+        col[h * M : (h + 1) * M, :] = jnp.transpose(line).astype(jnp.int32) - SL // 2
+    real = g_ref[0].astype(F32).reshape(K // 2 * L, P)
+    imag = g_ref[1].astype(F32).reshape(K // 2 * L, P)
+    g32[: K // 2 * L] = jnp.concatenate([real, -imag], axis=1)
+    g32[K // 2 * L :] = jnp.concatenate([imag, real], axis=1)
+    accbuf[...] = jnp.zeros_like(accbuf)
+    mag_p = jnp.abs(col[pl.ds(pl.multiple_of(me * P, P), P), :])
+    dims = (((0,), (0,)), ((), ()))
+
+    def tables():
+        quarter = SL // 4
+        lane = lax.broadcasted_iota(jnp.int32, (M, M), 1)
+        for h in range(2):
+            orders = col[h * M : (h + 1) * M, :]
+            for t in range(4):
+                at = slice(t * M, (t + 1) * M)
+                phase = orders * (t * P + lane % P)
+                for x in range(2):
+                    hi, lo = split(cos_of(phase + (x - lane // P) * quarter, SL))
+                    alpha_hi[h, x * M : (x + 1) * M, at] = hi
+                    alpha_lo[h, x * M : (x + 1) * M, at] = lo
+                phase = orders * ((t % 2) * M + lane)
+                hi, lo = split(cos_of(phase + (t // 2) * quarter, SL))
+                gamma_hi[h * M : (h + 1) * M, at] = hi
+                gamma_lo[h * M : (h + 1) * M, at] = lo
+
+    def r_copy(h, blk):
+        return pltpu.make_async_remote_copy(
+            src_ref=rs_send.at[h, blk], dst_ref=rs_recv.at[h, blk],
+            send_sem=r_send_sem.at[h, blk], recv_sem=r_recv_sem.at[h, blk],
+            device_id={"degree": 1 - deg}, device_id_type=MESH,
+        )
+
+    def compute(h, arrivals):
+        mag_m = jnp.abs(row_ref[h] - SL // 2)
+        most = jnp.maximum(mag_p, jnp.broadcast_to(mag_m, (P, M)))
+        most = jnp.concatenate([most, most], axis=0)
+
+        def chunk(c, carry):
+            arrivals(c)
+            for i in range(per):
+                step = c * per + i
+                b0, b1 = sbuf[2 * h, step], sbuf[2 * h + 1, step]
+                low = jnp.concatenate([b0[:, :P], b1[:, :P]], axis=1)
+                high = jnp.concatenate([b0[:, P:], b1[:, P:]], axis=1)
+                for part, scene in ((0, low), (1, high)):
+                    l = step + part * HL
+                    grip = g32[pl.ds(l, K, stride=L), :].astype(BF16)
+                    value = lax.dot_general(grip, scene, dims, preferred_element_type=F32)
+                    value = jnp.where(most <= deg * L + l, value, F32(0.0))
+                    prod[part, i] = value.astype(BF16)
+            w_copy(h, c).wait()
+
+            def rows(blk, carry):
+                at = pl.multiple_of(blk * ROWS, ROWS)
+
+                def degree_step(i, acc):
+                    acc = list(acc)
+                    for part in range(2):
+                        pr = prod[part, i, pl.ds(at, ROWS), :].astype(F32)
+                        pi = prod[part, i, pl.ds(at + P, ROWS), :].astype(F32)
+                        for b in range(NBETA):
+                            w = wbuf[h, part, c * per + i, b, pl.ds(at, ROWS), :].astype(F32)
+                            acc[2 * b] += pr * w
+                            acc[2 * b + 1] += pi * w
+                    return tuple(acc)
+
+                acc = tuple(accbuf[h, blk, n // 2, n % 2] for n in range(2 * NBETA))
+                acc = lax.fori_loop(0, per, degree_step, acc, unroll=2)
+                for n in range(2 * NBETA):
+                    accbuf[h, blk, n // 2, n % 2] = acc[n]
+
+                @pl.when(c == CHUNKS - 1)
+                def _():
+                    rs_send[h, blk] = accbuf[h, blk, pl.ds((1 - deg) * BO, BO)].astype(BF16)
+                    r_copy(h, blk).start()
+
+                return carry
+
+            return lax.fori_loop(0, blocks, rows, carry)
+
+        lax.fori_loop(0, CHUNKS, chunk, 0)
+
+    def alpha(h, blk):
+        r_copy(h, blk).wait_recv()
+        total = accbuf[h, blk, pl.ds(deg * BO, BO)] + rs_recv[h, blk].astype(F32)
+        total = jnp.concatenate(
+            [total[:, 0].reshape(BO * ROWS, M), total[:, 1].reshape(BO * ROWS, M)], axis=1
+        )
+        hi, lo = split(total)
+        value = jnp.dot(hi, alpha_hi[h], preferred_element_type=F32)
+        value += jnp.dot(hi, alpha_lo[h], preferred_element_type=F32)
+        value += jnp.dot(lo, alpha_hi[h], preferred_element_type=F32)
+        return value
+
+    across = lax.max(me - 1, 0) % 2
+    middle = (me == 1) | (me == 2)
+    other = me + 1 - 2 * across
+    beyond = other + 1 - 2 * across
+
+    def wait_block(block, c):
+        hop(block, c, me // 3).wait_recv()
+
+    def arrivals_first(c):
+        wait_block(near, c)
+
+        @pl.when(middle)
+        def _():
+            hop(near, c, across).start()
+            wait_block(other, c)
+            hop(other, c, 1 - across).start()
+
+    def arrivals_second(c):
+        @pl.when(middle)
+        def _():
+            wait_block(beyond, c)
+            hop(beyond, c, 1 - across).start()
+
+        @pl.when(jnp.logical_not(middle))
+        def _():
+            wait_block(second * 2, c)
+            wait_block(second * 2 + 1, c)
+
+    tables()
+    compute(first, arrivals_first)
+    compute(second, arrivals_second)
+
+    def x_copy(target, source, blk, off):
+        return pltpu.make_async_remote_copy(
+            src_ref=a_send.at[target, blk], dst_ref=a_recv.at[source, blk],
+            send_sem=x_send_sem.at[off, blk], recv_sem=x_recv_sem.at[off, blk],
+            device_id={"order": target}, device_id_type=MESH,
+        )
+
+    for blk in range(blocks):
+        halfacc[blk] = alpha(first, blk)
+    for blk in range(blocks):
+        value = (halfacc[blk] + alpha(second, blk)).astype(BF16)
+        for t in range(4):
+            a_send[t, blk] = value[:, t * M : (t + 1) * M]
+        for off in (2, 1, 3):
+            x_copy((me + off) % 4, me, blk, off).start()
+        a_recv[me, blk] = a_send[me, blk]
+
+    for blk in range(blocks):
+        for off in (1, 3, 2):
+            source = (me - off + 4) % 4
+            x_copy(source, source, blk, off).wait_recv()
+
+    score = jnp.zeros((BO * P, SL), F32)
+    got = [
+        jnp.concatenate(
+            [a_recv[z, blk, b * ROWS : (b + 1) * ROWS, :] for z in range(4) for blk in range(blocks)],
+            axis=0,
+        )
+        for b in range(BO)
+    ]
+    for x in range(2):
+        left = jnp.concatenate([piece[:, x * P : (x + 1) * P] for piece in got], axis=1)
+        for table in (gamma_hi, gamma_lo):
+            score += lax.dot_general(
+                left, table[:, x * SL : (x + 1) * SL], dims, preferred_element_type=F32
+            )
+    out_ref[0] = score.reshape(BO, P, SL)
+
+    for c in range(CHUNKS):
+        @pl.when(me < 3)
+        def _():
+            hop(me, c, 0, True).wait_send()
+
+        @pl.when(me > 0)
+        def _():
+            hop(me, c, 1, True).wait_send()
+
+        @pl.when(middle)
+        def _():
+            hop(near, c, across).wait_send()
+            hop(other, c, 1 - across).wait_send()
+            hop(beyond, c, 1 - across).wait_send()
+
+    for blk in range(blocks):
+        for off in (1, 2, 3):
+            x_copy((me + off) % 4, me, blk, off).wait_send()
+        r_copy(first, blk).wait_send()
+        r_copy(second, blk).wait_send()
+
+
+def fused_shards(scene_coeffs, site_ids, gripper_coeffs, order_table, wigner):
+    L, NBETA, P, SL = wigner.shape
+    M = SL // 2
+    K = 2 * scene_coeffs.shape[1]
+    BO = NBETA // 2
+    NB = P // ROWS
+    chosen = lax.dynamic_index_in_dim(scene_coeffs, site_ids[0], axis=4, keepdims=False)
+    s = jnp.transpose(chosen, (2, 0, 1, 3)).reshape(2, L // 2, K, P)
+    s = jnp.concatenate([s[0], s[1]], axis=-1)
+    vmem = pl.BlockSpec(memory_space=pltpu.VMEM)
+    return pl.pallas_call(
+        fused_kernel,
+        out_shape=jax.ShapeDtypeStruct((1, BO, P, SL), F32),
+        in_specs=[vmem, vmem, vmem, pl.BlockSpec(memory_space=pl.ANY)],
+        out_specs=vmem,
+        scratch_shapes=[
+            pltpu.VMEM((2, 2, L // 2, NBETA, P, M), BF16),
+            pltpu.VMEM((4, L // 2, K, 2 * P), BF16),
+            pltpu.VMEM((2, L // 2 // CHUNKS, 2 * P, M), BF16),
+            pltpu.VMEM((2, NB, NBETA, 2, ROWS, M), F32),
+            pltpu.VMEM((2, NB, BO, 2, ROWS, M), BF16),
+            pltpu.VMEM((2, NB, BO, 2, ROWS, M), BF16),
+            pltpu.VMEM((4, NB, BO * ROWS, M), BF16),
+            pltpu.VMEM((4, NB, BO * ROWS, M), BF16),
+            pltpu.VMEM((NB, BO * ROWS, 2 * SL), F32),
+            pltpu.VMEM((2, 2 * M, 2 * SL), BF16),
+            pltpu.VMEM((2, 2 * M, 2 * SL), BF16),
+            pltpu.VMEM((SL, 2 * SL), BF16),
+            pltpu.VMEM((SL, 2 * SL), BF16),
+            pltpu.VMEM((K * L, 2 * P), F32),
+            pltpu.VMEM((SL, M), jnp.int32),
+            pltpu.SemaphoreType.DMA((2, CHUNKS)),
+            pltpu.SemaphoreType.DMA((2, 4, CHUNKS)),
+            pltpu.SemaphoreType.DMA((4, CHUNKS)),
+            pltpu.SemaphoreType.DMA((2, NB)),
+            pltpu.SemaphoreType.DMA((2, NB)),
+            pltpu.SemaphoreType.DMA((4, NB)),
+            pltpu.SemaphoreType.DMA((4, NB)),
+        ],
+        compiler_params=pltpu.CompilerParams(
+            collective_id=0, has_side_effects=True, vmem_limit_bytes=48 * 1024 * 1024
+        ),
+    )(s, gripper_coeffs, order_table.reshape(2, 1, M), wigner.reshape(2, L // 2, NBETA, P, SL))
+
+
 def solution(mesh):
+    fits = mesh.shape["order"] == 4 and mesh.shape["degree"] == 2 and mesh.shape["site"] == 4
+    shards = fused_shards if fits else general_shards
     in_specs = (
         P(None, None, "degree", "order", None),
         P("site"),

time: 217 us -> 42.3 us (0.19)
  local copies, waits for them, and re-layouts: 105 us -> 6.25 us
  matrix products: 40.9 us -> 0 us
  Pallas kernels: 0 us -> 35 us
  waiting for transfers between devices: 30 us -> 0 us
  blocking collectives: 18.7 us -> 0 us
  between operations: 14.3 us -> 0.72 us
  other arithmetic: 5.92 us -> 0.15 us
    unnamed x10 -> x6, local copies, waits for them, and re-layouts: 53.9 us -> 2.5 us
    dot_general x6 -> x0, matrix products: 40.9 us -> none  [the longest x1 25.7 us: shards(): jnp.einsum('ylprs,lbpr->ysbpr', product, wigner, preferred_element_type=j...]
    pallas_call x0 -> x1, Pallas kernels: none -> 35 us  [fused_shards(): pl.pallas_call(fused_kernel, out_shape=jax.ShapeDtypeStruct((1, BO, P, SL...]
    all_to_all x1 -> x0, blocking collectives: 18.7 us -> none  [shards(): lax.all_to_all(stacked_parts, 'order', split_axis=4, concat_axis=3, tiled...]
    reduce_scatter x1 -> x0, waiting for transfers between devices: 18.3 us -> none  [shards(): lax.psum_scatter(partial_value, 'degree', scatter_dimension=2, tiled=True)]
    reshape x3 -> x0, local copies, waits for them, and re-layouts: 17.7 us -> none  [the longest x1 16 us: shards(): scene_coeffs.reshape(-1, cand_count)]
    another operation x4 -> x0, local copies, waits for them, and re-layouts: 15.7 us -> none
    transpose x1 -> x0, local copies, waits for them, and re-layouts: 14.2 us -> none  [shards(): jnp.einsum('ylprs,lbpr->ysbpr', product, wigner, preferred_element_type=j...]
  transfers between devices with their start and end apart: 2 -> 0, of which waited for: 2 -> 0; matrix products, arithmetic and copies ran while one was open for 17% -> 0% of each run, Pallas kernels for 0% -> 0%
where the time goes in v2:
time: 42.3 us; the launch traced here: 42.1 us
  Pallas kernels  35 us (83%)
  local copies, waits for them, and re-layouts  6.25 us (15%)
  between operations  0.72 us (2%)
    pallas_call x1, Pallas kernels, fused_shards(): pl.pallas_call(fused_kernel, out_shape=jax.ShapeDtypeStruct((1, BO, P, SL...  35 us
    dynamic_slice x1, local copies, waits for them, and re-layouts, fused_shards(): lax.dynamic_index_in_dim(scene_coeffs, site_ids[0], axis=4, keepdims=False)  3.51 us
    unnamed x6, local copies, waits for them, and re-layouts  2.5 us

profile of v2, /device:TPU:0, one launch (start us, length us, event | category | flops | bytes accessed | tf_op | source)
XLA Modules:
  0.0 42.1 jit_solution(8391144225670339985)
XLA Ops:
  0.7 3.5 %constant_dynamic-slice_fusion = bf16[2,16,64,64,1]{3,4,2,1,0:T(2,128)(2,1)S(1)} fusion(bf16[2,16,64,64,32]{3,4,2,1,0:T(8,128)(2,1)} %param.5, s32[]{:T(128)S(6)} %select_n.4), kind=kLoop, calls=%fused_computation.2 | loop fusion | bytes 524292 | tf_op jit(solution)/shard_map/jit(dynamic_index_in_dim)/dynamic_slice | solution.py:352
  4.2 0.1 copy.11
  4.3 0.1 copy.7
  4.4 0.1 copy.8
  4.5 0.1 pad_maximum_fusion.s_ref
  4.7 0.0 copy-start
  4.7 1.0 %copy-done = bf16[2,16,64,64]{3,2,1,0:T(8,128)(2,1)S(1)} copy-done((bf16[2,16,64,64]{3,2,1,0:T(8,128)(2,1)S(1)}, bf16[2,16,64,64]{3,2,1,0:T(8,128)(2,1)}, u32[]{:S(2)}) %copy-start) | copy-done | bytes 262168
  5.7 0.0 copy-start.1
  5.7 0.7 %copy-done.1 = s32[256]{0:T(256)S(1)} copy-done((s32[256]{0:T(256)S(1)}, s32[256]{0:T(256)}, u32[]{:S(2)}) %copy-start.1) | copy-done | bytes 1048
  6.4 35.0 %shard_map.55 = f32[1,4,64,256]{3,2,1,0:T(8,128)S(1)} custom-call(bf16[32,32,128]{2,1,0:T(8,128)(2,1)S(1)} %pad_maximum_fusion.s_ref, bf16[2,16,64,64]{3,2,1,0:T(8,128)(2,1)S(1)} %copy-done, s32[2,1,128]{2,1,0:T(1,128)S(1)} %bitcast.13, bf16[2,32,8,64,256]{4,3,2,1,0:T(8,128)(2,1)} %bitcast.14), custom_call_target="tpu_custom_call" | custom-call | tf_op jit(solution)/shard_map/pallas_call | solution.py:356
  41.4 0.7 %copy.14 = f32[1,4,64,256]{3,2,1,0:T(8,128)} copy(f32[1,4,64,256]{3,2,1,0:T(8,128)S(1)} %shard_map.55) | data formatting | bytes 524288
  (1 shorter events, 0.0 us)
Async XLA Ops:
  4.7 1.0 %copy-start = (bf16[2,16,64,64]{3,2,1,0:T(8,128)(2,1)S(1)}, bf16[2,16,64,64]{3,2,1,0:T(8,128)(2,1)}, u32[]{:S(2)}) copy-start(bf16[2,16,64,64]{3,2,1,0:T(8,128)(2,1)} %g_ref.1) | copy-start | bytes 786436
  5.7 0.7 %copy-start.1 = (s32[256]{0:T(256)S(1)}, s32[256]{0:T(256)}, u32[]{:S(2)}) copy-start(s32[256]{0:T(256)} %param.8) | copy-start | bytes 3076

commit v3 on v2

--- a/solution.py
+++ b/solution.py
@@ -79,6 +79,7 @@
 F32, BF16 = jnp.float32, jnp.bfloat16
 CHUNKS = 4
 ROWS = 16
+VMEM_LIMIT = 66633728
 
 
 def cos_of(index, count):
@@ -100,8 +101,8 @@
 def fused_kernel(
     s_ref, g_ref, row_ref, w_ref, out_ref,
     wbuf, sbuf, prod, accbuf, rs_send, rs_recv, a_send, a_recv, halfacc,
-    alpha_hi, alpha_lo, gamma_hi, gamma_lo, g32, col,
-    w_sem, s_send_sem, s_recv_sem, r_send_sem, r_recv_sem, x_send_sem, x_recv_sem,
+    alpha_hi, alpha_lo, gamma_hi, gamma_lo, g32, col, g_buf, row_buf,
+    in_sem, w_sem, s_send_sem, s_recv_sem, r_send_sem, r_recv_sem, x_send_sem, x_recv_sem,
 ):
     me = lax.axis_index("order")
     deg = lax.axis_index("degree")
@@ -128,6 +129,10 @@
         pl.semaphore_signal(barrier, 1, device_id={"order": (me + off) % 4}, device_id_type=MESH)
     pl.semaphore_signal(barrier, 1, device_id={"degree": 1 - deg}, device_id_type=MESH)
 
+    row_copy = pltpu.make_async_copy(row_ref, row_buf, in_sem.at[0])
+    g_copy = pltpu.make_async_copy(g_ref, g_buf, in_sem.at[1])
+    row_copy.start()
+    g_copy.start()
     for h in (first, second):
         for c in range(CHUNKS):
             w_copy(h, c).start()
@@ -152,13 +157,16 @@
         def _():
             hop(me, c, 1, True).start()
 
-    sbuf[me] = s_ref[...]
-
+    s_own = pltpu.make_async_copy(s_ref, sbuf.at[me], in_sem.at[2])
+    s_own.start()
+
+    row_copy.wait()
     for h in range(2):
-        line = jnp.broadcast_to(row_ref[h].astype(F32), (M, M))
+        line = jnp.broadcast_to(row_buf[h].astype(F32), (M, M))
         col[h * M : (h + 1) * M, :] = jnp.transpose(line).astype(jnp.int32) - SL // 2
-    real = g_ref[0].astype(F32).reshape(K // 2 * L, P)
-    imag = g_ref[1].astype(F32).reshape(K // 2 * L, P)
+    g_copy.wait()
+    real = g_buf[0].astype(F32).reshape(K // 2 * L, P)
+    imag = g_buf[1].astype(F32).reshape(K // 2 * L, P)
     g32[: K // 2 * L] = jnp.concatenate([real, -imag], axis=1)
     g32[K // 2 * L :] = jnp.concatenate([imag, real], axis=1)
     accbuf[...] = jnp.zeros_like(accbuf)
@@ -167,38 +175,52 @@
 
     def tables():
         quarter = SL // 4
-        lane = lax.broadcasted_iota(jnp.int32, (M, M), 1)
-        for h in range(2):
-            orders = col[h * M : (h + 1) * M, :]
+        lane = lax.broadcasted_iota(jnp.int32, (P, M), 1)
+        for q in range(4):
+            orders = col[q * P : (q + 1) * P, :]
             for t in range(4):
                 at = slice(t * M, (t + 1) * M)
                 phase = orders * (t * P + lane % P)
                 for x in range(2):
                     hi, lo = split(cos_of(phase + (x - lane // P) * quarter, SL))
-                    alpha_hi[h, x * M : (x + 1) * M, at] = hi
-                    alpha_lo[h, x * M : (x + 1) * M, at] = lo
+                    alpha_hi[q, x * P : (x + 1) * P, at] = hi
+                    alpha_lo[q, x * P : (x + 1) * P, at] = lo
                 phase = orders * ((t % 2) * M + lane)
                 hi, lo = split(cos_of(phase + (t // 2) * quarter, SL))
-                gamma_hi[h * M : (h + 1) * M, at] = hi
-                gamma_lo[h * M : (h + 1) * M, at] = lo
-
-    def r_copy(h, blk):
+                gamma_hi[q * P : (q + 1) * P, at] = hi
+                gamma_lo[q * P : (q + 1) * P, at] = lo
+
+    def r_copy(q, blk):
         return pltpu.make_async_remote_copy(
-            src_ref=rs_send.at[h, blk], dst_ref=rs_recv.at[h, blk],
-            send_sem=r_send_sem.at[h, blk], recv_sem=r_recv_sem.at[h, blk],
+            src_ref=rs_send.at[q, blk], dst_ref=rs_recv.at[q, blk],
+            send_sem=r_send_sem.at[q, blk], recv_sem=r_recv_sem.at[q, blk],
             device_id={"degree": 1 - deg}, device_id_type=MESH,
         )
 
-    def compute(h, arrivals):
-        mag_m = jnp.abs(row_ref[h] - SL // 2)
+    def packed(q, blk, who):
+        held = accbuf[q // 2, blk, pl.ds(who * BO, BO)]
+        upper = q % 2 == 1
+        parts = [jnp.where(upper, held[:, x, :, P:], held[:, x, :, :P]) for x in range(2)]
+        return jnp.concatenate(parts, axis=-1)
+
+    def compute(h, quarters, arrivals, passing=None):
+        wide = len(quarters) == 2
+        only = quarters[0] % 2
+        lanes = lax.broadcasted_iota(jnp.int32, (2 * P, M), 1) // P
+        mag_m = jnp.abs(row_buf[h] - SL // 2)
         most = jnp.maximum(mag_p, jnp.broadcast_to(mag_m, (P, M)))
         most = jnp.concatenate([most, most], axis=0)
+        if not wide:
+            most = jnp.where(lanes == only, most, SL)
 
         def chunk(c, carry):
             arrivals(c)
             for i in range(per):
                 step = c * per + i
-                b0, b1 = sbuf[2 * h, step], sbuf[2 * h + 1, step]
+                if wide:
+                    b0, b1 = sbuf[2 * h, step], sbuf[2 * h + 1, step]
+                else:
+                    b0 = b1 = sbuf[quarters[0], step]
                 low = jnp.concatenate([b0[:, :P], b1[:, :P]], axis=1)
                 high = jnp.concatenate([b0[:, P:], b1[:, P:]], axis=1)
                 for part, scene in ((0, low), (1, high)):
@@ -207,7 +229,8 @@
                     value = lax.dot_general(grip, scene, dims, preferred_element_type=F32)
                     value = jnp.where(most <= deg * L + l, value, F32(0.0))
                     prod[part, i] = value.astype(BF16)
-            w_copy(h, c).wait()
+            if passing is None or passing is arrivals_after_a:
+                w_copy(h, c).wait()
 
             def rows(blk, carry):
                 at = pl.multiple_of(blk * ROWS, ROWS)
@@ -230,25 +253,30 @@
 
                 @pl.when(c == CHUNKS - 1)
                 def _():
-                    rs_send[h, blk] = accbuf[h, blk, pl.ds((1 - deg) * BO, BO)].astype(BF16)
-                    r_copy(h, blk).start()
+                    for q in quarters:
+                        rs_send[q, blk] = packed(q, blk, 1 - deg).astype(BF16)
+                        r_copy(q, blk).start()
 
                 return carry
 
-            return lax.fori_loop(0, blocks, rows, carry)
+            lax.fori_loop(0, blocks, rows, 0)
+            if passing is not None:
+                passing(c)
+            return carry
 
         lax.fori_loop(0, CHUNKS, chunk, 0)
 
-    def alpha(h, blk):
-        r_copy(h, blk).wait_recv()
-        total = accbuf[h, blk, pl.ds(deg * BO, BO)] + rs_recv[h, blk].astype(F32)
-        total = jnp.concatenate(
-            [total[:, 0].reshape(BO * ROWS, M), total[:, 1].reshape(BO * ROWS, M)], axis=1
-        )
+    def alpha(q, blks):
+        pieces = []
+        for blk in blks:
+            r_copy(q, blk).wait_recv()
+            piece = packed(q, blk, deg) + rs_recv[q, blk].astype(F32)
+            pieces.append(piece.reshape(BO * ROWS, M))
+        total = pieces[0] if len(pieces) == 1 else jnp.concatenate(pieces, axis=0)
         hi, lo = split(total)
-        value = jnp.dot(hi, alpha_hi[h], preferred_element_type=F32)
-        value += jnp.dot(hi, alpha_lo[h], preferred_element_type=F32)
-        value += jnp.dot(lo, alpha_hi[h], preferred_element_type=F32)
+        value = jnp.dot(hi, alpha_hi[q], preferred_element_type=F32)
+        value += jnp.dot(hi, alpha_lo[q], preferred_element_type=F32)
+        value += jnp.dot(lo, alpha_hi[q], preferred_element_type=F32)
         return value
 
     across = lax.max(me - 1, 0) % 2
@@ -268,20 +296,33 @@
             wait_block(other, c)
             hop(other, c, 1 - across).start()
 
-    def arrivals_second(c):
+    early = jnp.where(me < 2, 2, 1)
+    late = jnp.where(me < 2, 3, 0)
+
+    def arrivals_a(c):
+        @pl.when(jnp.logical_not(middle))
+        def _():
+            wait_block(early, c)
+
+    def arrivals_after_a(c):
         @pl.when(middle)
         def _():
             wait_block(beyond, c)
             hop(beyond, c, 1 - across).start()
 
+    def arrivals_b(c):
         @pl.when(jnp.logical_not(middle))
         def _():
-            wait_block(second * 2, c)
-            wait_block(second * 2 + 1, c)
-
+            wait_block(late, c)
+
+    every = tuple(range(blocks))
     tables()
-    compute(first, arrivals_first)
-    compute(second, arrivals_second)
+    s_own.wait()
+    compute(first, (first * 2, first * 2 + 1), arrivals_first)
+    compute(second, (early,), arrivals_a, arrivals_after_a)
+    halfacc[...] = alpha(first * 2, every) + alpha(first * 2 + 1, every)
+    compute(second, (late,), arrivals_b, lambda c: None)
+    halfacc[...] += alpha(early, every)
 
     def x_copy(target, source, blk, off):
         return pltpu.make_async_remote_copy(
@@ -291,9 +332,8 @@
         )
 
     for blk in range(blocks):
-        halfacc[blk] = alpha(first, blk)
-    for blk in range(blocks):
-        value = (halfacc[blk] + alpha(second, blk)).astype(BF16)
+        mine = slice(blk * BO * ROWS, (blk + 1) * BO * ROWS)
+        value = (halfacc[mine, :] + alpha(late, (blk,))).astype(BF16)
         for t in range(4):
             a_send[t, blk] = value[:, t * M : (t + 1) * M]
         for off in (2, 1, 3):
@@ -339,8 +379,8 @@
     for blk in range(blocks):
         for off in (1, 2, 3):
             x_copy((me + off) % 4, me, blk, off).wait_send()
-        r_copy(first, blk).wait_send()
-        r_copy(second, blk).wait_send()
+        for q in range(4):
+            r_copy(q, blk).wait_send()
 
 
 def fused_shards(scene_coeffs, site_ids, gripper_coeffs, order_table, wigner):
@@ -353,37 +393,41 @@
     s = jnp.transpose(chosen, (2, 0, 1, 3)).reshape(2, L // 2, K, P)
     s = jnp.concatenate([s[0], s[1]], axis=-1)
     vmem = pl.BlockSpec(memory_space=pltpu.VMEM)
+    hbm = pl.BlockSpec(memory_space=pltpu.HBM)
     return pl.pallas_call(
         fused_kernel,
         out_shape=jax.ShapeDtypeStruct((1, BO, P, SL), F32),
-        in_specs=[vmem, vmem, vmem, pl.BlockSpec(memory_space=pl.ANY)],
+        in_specs=[hbm, hbm, hbm, hbm],
         out_specs=vmem,
         scratch_shapes=[
             pltpu.VMEM((2, 2, L // 2, NBETA, P, M), BF16),
             pltpu.VMEM((4, L // 2, K, 2 * P), BF16),
             pltpu.VMEM((2, L // 2 // CHUNKS, 2 * P, M), BF16),
             pltpu.VMEM((2, NB, NBETA, 2, ROWS, M), F32),
-            pltpu.VMEM((2, NB, BO, 2, ROWS, M), BF16),
-            pltpu.VMEM((2, NB, BO, 2, ROWS, M), BF16),
+            pltpu.VMEM((4, NB, BO, ROWS, M), BF16),
+            pltpu.VMEM((4, NB, BO, ROWS, M), BF16),
             pltpu.VMEM((4, NB, BO * ROWS, M), BF16),
             pltpu.VMEM((4, NB, BO * ROWS, M), BF16),
-            pltpu.VMEM((NB, BO * ROWS, 2 * SL), F32),
-            pltpu.VMEM((2, 2 * M, 2 * SL), BF16),
-            pltpu.VMEM((2, 2 * M, 2 * SL), BF16),
+            pltpu.VMEM((NB * BO * ROWS, 2 * SL), F32),
+            pltpu.VMEM((4, M, 2 * SL), BF16),
+            pltpu.VMEM((4, M, 2 * SL), BF16),
             pltpu.VMEM((SL, 2 * SL), BF16),
             pltpu.VMEM((SL, 2 * SL), BF16),
             pltpu.VMEM((K * L, 2 * P), F32),
             pltpu.VMEM((SL, M), jnp.int32),
+            pltpu.VMEM((2, K // 2, L, P), BF16),
+            pltpu.VMEM((2, 1, M), jnp.int32),
+            pltpu.SemaphoreType.DMA((3,)),
             pltpu.SemaphoreType.DMA((2, CHUNKS)),
             pltpu.SemaphoreType.DMA((2, 4, CHUNKS)),
             pltpu.SemaphoreType.DMA((4, CHUNKS)),
-            pltpu.SemaphoreType.DMA((2, NB)),
-            pltpu.SemaphoreType.DMA((2, NB)),
+            pltpu.SemaphoreType.DMA((4, NB)),
+            pltpu.SemaphoreType.DMA((4, NB)),
             pltpu.SemaphoreType.DMA((4, NB)),
             pltpu.SemaphoreType.DMA((4, NB)),
         ],
         compiler_params=pltpu.CompilerParams(
-            collective_id=0, has_side_effects=True, vmem_limit_bytes=48 * 1024 * 1024
+            collective_id=0, has_side_effects=True, vmem_limit_bytes=VMEM_LIMIT
         ),
     )(s, gripper_coeffs, order_table.reshape(2, 1, M), wigner.reshape(2, L // 2, NBETA, P, SL))
 

time: 42.3 us -> 48.7 us (1.15)
  Pallas kernels: 35 us -> 41.5 us
  local copies, waits for them, and re-layouts: 6.25 us -> 5.51 us
  other arithmetic: 0.15 us -> 0.85 us
    pallas_call x1, Pallas kernels: 35 us -> 41.5 us  [fused_shards(): pl.pallas_call(fused_kernel, out_shape=jax.ShapeDtypeStruct((1, BO, P, SL...]
    unnamed x6 -> x2, local copies, waits for them, and re-layouts: 2.5 us -> 1.75 us
    concatenate x1, other arithmetic: 0.15 us -> 0.85 us  [fused_shards(): s = jnp.concatenate([s[0], s[1]], axis=-1)]
where the time goes in v3:
time: 48.7 us; the launch traced here: 48.6 us
  Pallas kernels  41.5 us (85%)
  local copies, waits for them, and re-layouts  5.51 us (11%)
  other arithmetic  0.85 us (2%)
  between operations  0.7 us (1%)
    pallas_call x1, Pallas kernels, fused_shards(): pl.pallas_call(fused_kernel, out_shape=jax.ShapeDtypeStruct((1, BO, P, SL...  41.5 us
    dynamic_slice x1, local copies, waits for them, and re-layouts, fused_shards(): lax.dynamic_index_in_dim(scene_coeffs, site_ids[0], axis=4, keepdims=False)  3.51 us
    unnamed x2, local copies, waits for them, and re-layouts  1.75 us

profile of v3, /device:TPU:0, one launch (start us, length us, event | category | flops | bytes accessed | tf_op | source)
XLA Modules:
  0.0 48.6 jit_solution(1949240173990216834)
XLA Ops:
  0.7 3.5 %constant_dynamic-slice_fusion = bf16[2,16,64,64,1]{3,4,2,1,0:T(2,128)(2,1)S(1)} fusion(bf16[2,16,64,64,32]{3,4,2,1,0:T(8,128)(2,1)} %param.5, s32[]{:T(128)S(6)} %select_n.4), kind=kLoop, calls=%fused_computation.2 | loop fusion | bytes 524292 | tf_op jit(solution)/shard_map/jit(dynamic_index_in_dim)/dynamic_slice | solution.py:392
  4.2 0.1 copy.11
  4.3 0.1 copy.7
  4.4 0.1 copy.8
  4.5 0.9 %pad_maximum_fusion.s_ref = bf16[32,32,128]{2,1,0:T(8,128)(2,1)} fusion(bf16[32,32,64]{2,1,0:T(8,128)(2,1)S(1)} %bitcast.16, bf16[32,32,64]{2,1,0:T(8,128)(2,1)S(1)} %bitcast.15), kind=kLoop, calls=%fused_computation.1 | loop fusion | flops 524288 | bytes 524288 | tf_op jit(solution)/shard_map/concatenate | solution.py:394
  5.4 41.5 %shard_map.55 = f32[1,4,64,256]{3,2,1,0:T(8,128)} custom-call(bf16[32,32,128]{2,1,0:T(8,128)(2,1)} %pad_maximum_fusion.s_ref, bf16[2,16,64,64]{3,2,1,0:T(8,128)(2,1)} %g_ref.1, s32[2,1,128]{2,1,0:T(1,128)} %bitcast.17, bf16[2,32,8,64,256]{4,3,2,1,0:T(8,128)(2,1)} %bitcast.13), custom_call_target="tpu_custom_call" | custom-call | tf_op jit(solution)/shard_map/pallas_call | solution.py:397
  46.9 1.7 %copy.14 = f32[1,4,64,256]{3,2,1,0:T(8,128)} copy(f32[1,4,64,256]{3,2,1,0:T(8,128)} %shard_map.55) | data formatting | bytes 524288
  (1 shorter events, 0.0 us)

commit v4 on v2

--- a/solution.py
+++ b/solution.py
@@ -77,7 +77,7 @@
 
 MESH = pl.DeviceIdType.MESH
 F32, BF16 = jnp.float32, jnp.bfloat16
-CHUNKS = 4
+CHUNKS = 8
 ROWS = 16
 
 

time: 42.3 us -> 43.4 us (1.026)
  Pallas kernels: 35 us -> 36.1 us
    pallas_call x1, Pallas kernels: 35 us -> 36.1 us  [fused_shards(): pl.pallas_call(fused_kernel, out_shape=jax.ShapeDtypeStruct((1, BO, P, SL...]
where the time goes in v4:
time: 43.4 us; the launch traced here: 43.2 us
  Pallas kernels  36.1 us (83%)
  local copies, waits for them, and re-layouts  6.25 us (14%)
  between operations  0.72 us (2%)
    pallas_call x1, Pallas kernels, fused_shards(): pl.pallas_call(fused_kernel, out_shape=jax.ShapeDtypeStruct((1, BO, P, SL...  36.1 us
    dynamic_slice x1, local copies, waits for them, and re-layouts, fused_shards(): lax.dynamic_index_in_dim(scene_coeffs, site_ids[0], axis=4, keepdims=False)  3.51 us
    unnamed x6, local copies, waits for them, and re-layouts  2.5 us

profile of v4, /device:TPU:0, one launch (start us, length us, event | category | flops | bytes accessed | tf_op | source)
XLA Modules:
  0.0 43.2 jit_solution(4830035742680553520)
XLA Ops:
  0.7 3.5 %constant_dynamic-slice_fusion = bf16[2,16,64,64,1]{3,4,2,1,0:T(2,128)(2,1)S(1)} fusion(bf16[2,16,64,64,32]{3,4,2,1,0:T(8,128)(2,1)} %param.5, s32[]{:T(128)S(6)} %select_n.4), kind=kLoop, calls=%fused_computation.2 | loop fusion | bytes 524292 | tf_op jit(solution)/shard_map/jit(dynamic_index_in_dim)/dynamic_slice | solution.py:352
  4.2 0.1 copy.11
  4.3 0.1 copy.7
  4.4 0.1 copy.8
  4.5 0.1 pad_maximum_fusion.s_ref
  4.7 0.0 copy-start
  4.7 1.0 %copy-done = bf16[2,16,64,64]{3,2,1,0:T(8,128)(2,1)S(1)} copy-done((bf16[2,16,64,64]{3,2,1,0:T(8,128)(2,1)S(1)}, bf16[2,16,64,64]{3,2,1,0:T(8,128)(2,1)}, u32[]{:S(2)}) %copy-start) | copy-done | bytes 262168
  5.7 0.0 copy-start.1
  5.7 0.7 %copy-done.1 = s32[256]{0:T(256)S(1)} copy-done((s32[256]{0:T(256)S(1)}, s32[256]{0:T(256)}, u32[]{:S(2)}) %copy-start.1) | copy-done | bytes 1048
  6.4 36.1 %shard_map.55 = f32[1,4,64,256]{3,2,1,0:T(8,128)S(1)} custom-call(bf16[32,32,128]{2,1,0:T(8,128)(2,1)S(1)} %pad_maximum_fusion.s_ref, bf16[2,16,64,64]{3,2,1,0:T(8,128)(2,1)S(1)} %copy-done, s32[2,1,128]{2,1,0:T(1,128)S(1)} %bitcast.13, bf16[2,32,8,64,256]{4,3,2,1,0:T(8,128)(2,1)} %bitcast.14), custom_call_target="tpu_custom_call" | custom-call | tf_op jit(solution)/shard_map/pallas_call | solution.py:356
  42.5 0.7 %copy.14 = f32[1,4,64,256]{3,2,1,0:T(8,128)} copy(f32[1,4,64,256]{3,2,1,0:T(8,128)S(1)} %shard_map.55) | data formatting | bytes 524288
  (1 shorter events, 0.0 us)
Async XLA Ops:
  4.7 1.0 %copy-start = (bf16[2,16,64,64]{3,2,1,0:T(8,128)(2,1)S(1)}, bf16[2,16,64,64]{3,2,1,0:T(8,128)(2,1)}, u32[]{:S(2)}) copy-start(bf16[2,16,64,64]{3,2,1,0:T(8,128)(2,1)} %g_ref.1) | copy-start | bytes 786436
  5.7 0.7 %copy-start.1 = (s32[256]{0:T(256)S(1)}, s32[256]{0:T(256)}, u32[]{:S(2)}) copy-start(s32[256]{0:T(256)} %param.8) | copy-start | bytes 3076
